TPU v7x, 128 devices: a whole 4x4x4 slice. The times are simulated.
128 devices in a mesh: row: 8 (over z, y_lo), col: 16 (over y_hi, x, core).
Axes of the slice: x: 4, y: 4 (y_hi: 2, y_lo: 2; y = y_hi * 2 + y_lo), z: 4, core: 2. Of those that a mesh axis runs over, the one named last changes fastest.
Arguments:
- spectra: bfloat16 [2048, 256, 512], P(('row', 'col')), may hold values from 0.05 to 20000
- sensor_ids: int32 [2048, 1], P(('row', 'col')), may hold values from 0 to 255, as said below
- permutation: int32 [2048], P(('row', 'col')), may hold values from 0 to 2047, as said below
- w_enc1: bfloat16 [2048, 256], replicated, may hold values from -0.125 to 0.125
- w_enc2: bfloat16 [1024, 256], replicated, may hold values from -0.1875 to 0.1875
- w_dec1: bfloat16 [256, 1024], replicated, may hold values from -0.25 to 0.25
- w_dec2: bfloat16 [256, 2048], replicated, may hold values from -0.25 to 0.25
Outputs:
- grad_enc1: float32 [2048, 256], replicated
- grad_enc2: float32 [1024, 256], replicated
- grad_dec1: float32 [256, 1024], replicated
- grad_dec2: float32 [256, 2048], replicated
Inputs may be any that keep to these rules, and one draw needn't show every extreme that they name: `sensor_ids`: every sensor from 0 to 255 recorded exactly 8 windows. A permutation of all slots; the 16 windows of the ingest device with indices (a, b) go to 16 different trainers, one to each trainer whose col index c has c // 2 = a; each trainer thus receives one window from each ingest device of one row index.
All inputs are finite; a program needn't handle non-finite values.
Results may differ from a plain program's by a relative error of at most 0.004.
Values may be sent and summed in bfloat16 or wider, within the bound.
No kernel may reach another device: no remote copies, remote signals or barrier semaphores. Data moves between devices by JAX's collectives and lax.ppermute only.
A program may use at most 192 MiB of HBM per device.

v0:
```python
import jax
import jax.numpy as jnp
from jax import lax
from jax.sharding import PartitionSpec as P

WIN_SENSOR = 8
EPS = 1e-05


def frame_taps(values):
    windows, length, channels = values.shape
    padded = jnp.pad(values, ((0, 0), (1, 1), (0, 0)))
    paired = padded.reshape(windows, length // 2 + 1, 2 * channels)
    return jnp.concatenate([paired[:, :-1], paired[:, 1:]], axis=2)


def fold_taps(stacked):
    windows, length, columns = stacked.shape
    channels = columns // 4
    pieces = stacked.reshape(windows, length, 4, channels)
    blank = jnp.zeros((windows, 1, channels), stacked.dtype)
    even_rows = pieces[:, :, 1] + jnp.concatenate([blank, pieces[:, :-1, 3]], axis=1)
    odd_rows = pieces[:, :, 2] + jnp.concatenate([pieces[:, 1:, 0], blank], axis=1)
    return jnp.stack([even_rows, odd_rows], axis=2).reshape(windows, 2 * length, channels)


def silu_slope(values):
    logistic = jax.nn.sigmoid(values)
    return logistic * (1.0 + values * (1.0 - logistic))


def forward_dot(values, weight):
    flat = values.reshape(-1, values.shape[-1])
    result = jnp.dot(flat, weight, preferred_element_type=jnp.float32)
    return result.reshape(values.shape[:-1] + (weight.shape[1],))


def backward_dot(values, weight):
    flat = values.reshape(-1, values.shape[-1])
    result = lax.dot_general(
        flat, weight, (((1,), (1,)), ((), ())), preferred_element_type=jnp.float32
    )
    return result.reshape(values.shape[:-1] + (weight.shape[0],))


def sensor_table(sensor_col, sensor_total):
    return (sensor_col[:, None] == jnp.arange(sensor_total, dtype=jnp.int32)[None, :]).astype(
        jnp.float32
    )


def standardize(log_power, table, center, factor):
    shift = jnp.dot(table, center, precision=lax.Precision.HIGHEST)
    stretch = jnp.dot(table, factor, precision=lax.Precision.HIGHEST)
    return ((log_power - shift[:, None, :]) * stretch[:, None, :]).astype(jnp.bfloat16)


def layer_sum(left, right):
    left_flat = left.reshape(-1, left.shape[-1])
    right_flat = right.reshape(-1, right.shape[-1])
    gradient = jnp.einsum("rk,ro->ko", left_flat, right_flat, preferred_element_type=jnp.float32)
    return gradient


def local(spectra, sensor_ids, permutation, w_enc1, w_enc2, w_dec1, w_dec2):
    window_count = spectra.shape[0]
    frame_count = spectra.shape[1]
    row_count = lax.axis_size("row")
    col_count = lax.axis_size("col")
    total_windows = window_count * row_count * col_count
    sensor_total = total_windows // WIN_SENSOR
    sensor_col = sensor_ids[:, 0]
    table = sensor_table(sensor_col, sensor_total)
    log_power = jnp.log1p(spectra.astype(jnp.float32))
    win_sums = jnp.sum(log_power, axis=1)
    win_squares = jnp.sum(log_power * log_power, axis=1)
    totals = jnp.einsum("ws,wb->sb", table, win_sums, precision=lax.Precision.HIGHEST)
    squares = jnp.einsum("ws,wb->sb", table, win_squares, precision=lax.Precision.HIGHEST)
    counts = jnp.sum(table, axis=0) * frame_count
    totals, squares, counts = lax.psum((totals, squares, counts), ("row", "col"))
    center = totals / counts[:, None]
    factor = lax.rsqrt(squares / counts[:, None] - center * center + EPS)
    payload = standardize(log_power, table, center, factor)
    labels = jnp.stack([permutation, sensor_col], axis=1)
    positions = jnp.arange(window_count, dtype=jnp.int32)
    ranking = jnp.argsort(labels[:, 0] // col_count // col_count * col_count + positions)
    payload, labels = (
        lax.all_to_all(payload[ranking], "row", split_axis=0, concat_axis=0, tiled=True),
        lax.all_to_all(labels[ranking], "row", split_axis=0, concat_axis=0, tiled=True),
    )
    ranking = jnp.argsort(labels[:, 0] // col_count % col_count)
    payload, labels = (
        lax.all_to_all(payload[ranking], "col", split_axis=0, concat_axis=0, tiled=True),
        lax.all_to_all(labels[ranking], "col", split_axis=0, concat_axis=0, tiled=True),
    )
    stem_taps = frame_taps(payload)
    enc1_pre = forward_dot(stem_taps, w_enc1)
    middle = jnp.mean(enc1_pre, axis=(0, 1))
    variance = jnp.mean(jnp.square(enc1_pre - middle), axis=(0, 1))
    inverse = lax.rsqrt(variance + EPS)
    enc1_hat = (enc1_pre - middle) * inverse
    enc1_out = jax.nn.silu(enc1_hat).astype(jnp.bfloat16)
    mid_taps = frame_taps(enc1_out)
    enc2_pre = forward_dot(mid_taps, w_enc2)
    enc2_out = jax.nn.silu(enc2_pre).astype(jnp.bfloat16)
    dec1_pre = fold_taps(forward_dot(enc2_out, w_dec1))
    dec1_out = jax.nn.silu(dec1_pre).astype(jnp.bfloat16)
    rebuilt = fold_taps(forward_dot(dec1_out, w_dec2))
    delta_out = ((rebuilt - payload.astype(jnp.float32)) / total_windows).astype(jnp.bfloat16)
    out_taps = frame_taps(delta_out)
    grad_dec2 = layer_sum(dec1_out, out_taps)
    delta_dec1 = (backward_dot(out_taps, w_dec2) * silu_slope(dec1_pre)).astype(jnp.bfloat16)
    dec_taps = frame_taps(delta_dec1)
    grad_dec1 = layer_sum(enc2_out, dec_taps)
    delta_enc2 = (backward_dot(dec_taps, w_dec1) * silu_slope(enc2_pre)).astype(jnp.bfloat16)
    grad_enc2 = layer_sum(mid_taps, delta_enc2)
    back_enc1 = fold_taps(backward_dot(delta_enc2, w_enc2)) * silu_slope(enc1_hat)
    first_mean = jnp.mean(back_enc1, axis=(0, 1))
    second_mean = jnp.mean(back_enc1 * enc1_hat, axis=(0, 1))
    delta_enc1 = ((back_enc1 - first_mean - enc1_hat * second_mean) * inverse).astype(jnp.bfloat16)
    grad_enc1 = layer_sum(stem_taps, delta_enc1)
    grad_enc1, grad_enc2, grad_dec1, grad_dec2 = lax.psum(
        (grad_enc1, grad_enc2, grad_dec1, grad_dec2), ("row", "col")
    )
    return (grad_enc1, grad_enc2, grad_dec1, grad_dec2)


def solution(mesh):
    return jax.shard_map(
        local,
        mesh=mesh,
        in_specs=(
            P(("row", "col"), None, None),
            P(("row", "col"), None),
            P(("row", "col")),
            P(),
            P(),
            P(),
            P(),
        ),
        out_specs=(P(), P(), P(), P()),
        check_vma=False,
    )
```

profile of v0, /device:TPU:1, one launch (start us, length us, event | category | flops | bytes accessed | tf_op | source)
XLA Modules:
  0.0 608.6 jit_solution(8705638095930346824)
XLA Ops:
  7.2 5.9 fusion.2
  18.4 6.9 %all-to-all-start.1 = ((s32[8,2,2]{1,2,0:T(2,128)}), s32[8,2,2]{1,2,0:T(2,128)S(1)}, u32[]{:S(2)}, u32[]{:S(2)}) async-start(s32[8,2,2]{1,2,0:T(2,128)} %copy.99), calls=%async_computation.1 | async-start | bytes 16384 | tf_op jit(solution)/shard_map/all_to_all | solution.py:89
  25.4 67.2 %psum.50 = f32[256]{0:T(256)S(1)} all-reduce(f32[256]{0:T(256)S(1)} %broadcast_multiply_fusion.3), channel_id=1, replica_groups=mesh['row'=8,'col'=16] {'row','col'}, use_global_device_ids=true, to_apply=%region_3.0 | all-reduce | flops 256 | bytes 2048 | tf_op jit(solution)/shard_map/psum | solution.py:80
  92.6 74.5 %all-reduce.17.cloned.1.call-done = (f32[256,512]{1,0:T(8,128)}, f32[256,512]{1,0:T(8,128)}) async-done(((f32[256,512]{1,0:T(8,128)}, f32[256,512]{1,0:T(8,128)}), (f32[256,512]{1,0:T(8,128)}, f32[256,512]{1,0:T(8,128)})) %all-reduce.17.cloned.1.call-update) | async-done | bytes 1048592 | tf_op jit(solution)/shard_map/psum | solution.py:80
  170.4 5.4 multiply_convert_fusion
  175.8 4.9 gather_fusion
  180.7 4.6 all-to-all-start
  186.7 48.3 %all-to-all-done = bf16[16,256,512]{2,1,0:T(8,128)(2,1)} async-done(((bf16[16,256,512]{2,1,0:T(8,128)(2,1)}), bf16[16,256,512]{2,1,0:T(8,128)(2,1)}, u32[]{:S(2)}, u32[]{:S(2)}) %all-to-all-start) | async-done | bytes 4194336 | tf_op jit(solution)/shard_map/all_to_all | solution.py:88
  234.9 5.0 gather_fusion.2
  239.9 6.1 %all-to-all-start.2 = ((bf16[16,256,512]{2,1,0:T(8,128)(2,1)}), bf16[16,256,512]{2,1,0:T(8,128)(2,1)}, u32[]{:S(2)}, u32[]{:S(2)}) async-start(bf16[16,256,512]{2,1,0:T(8,128)(2,1)} %gather_fusion.2), calls=%async_computation.2 | async-start | bytes 8388608 | tf_op jit(solution)/shard_map/all_to_all | solution.py:93
  248.6 53.3 %all-to-all-done.2 = bf16[16,256,512]{2,1,0:T(8,128)(2,1)} async-done(((bf16[16,256,512]{2,1,0:T(8,128)(2,1)}), bf16[16,256,512]{2,1,0:T(8,128)(2,1)}, u32[]{:S(2)}, u32[]{:S(2)}) %all-to-all-start.2) | async-done | bytes 4194336 | tf_op jit(solution)/shard_map/all_to_all | solution.py:93
  301.9 5.9 pad.20
  307.9 7.2 %reshape.92 = bf16[16,129,1024]{2,1,0:T(8,128)(2,1)} reshape(bf16[16,258,512]{2,1,0:T(8,128)(2,1)} %pad.20) | data formatting | bytes 8454144 | tf_op jit(solution)/shard_map/reshape | solution.py:13
  315.1 4.4 fusion.66
  344.7 4.8 slice_bitcast_fusion.2
  352.9 11.7 %fusion.10 = (f32[16,128,1,512]{3,1,0,2:T(8,128)}, f32[16,128,1,512]{3,1,0,2:T(8,128)}) fusion(f32[16,128,4,512]{3,1,2,0:T(8,128)} %copy-done.2, f32[16,127,512]{2,1,0:T(8,128)} %get-tuple-element.20, f32[16,127,512]{2,1,0:T(8,128)} %get-tuple-element.21), kind=kLoop, calls=%fused_computation.24 | loop fusion | flops 2097152 | bytes 25100288 | tf_op jit(solution)/shard_map/stack | solution.py:24
  364.6 4.5 pad_maximum_fusion.1
  369.1 4.9 copy.111
  374.0 10.0 %fusion.1 = bf16[16,256,512]{2,1,0:T(8,128)(2,1)} fusion(f32[16,256,512]{2,0,1:T(8,128)S(1)} %bitcast.146, bf16[16,256,512]{2,1,0:T(8,128)(2,1)} %all-to-all-done.2), kind=kLoop, calls=%fused_computation.8 | loop fusion | flops 8388608 | bytes 16777216 | tf_op jit(solution)/shard_map/convert_element_type | solution.py:109
  384.0 5.9 pad.22
  389.9 7.2 %reshape.95 = bf16[16,129,1024]{2,1,0:T(8,128)(2,1)} reshape(bf16[16,258,512]{2,1,0:T(8,128)(2,1)} %pad.22) | data formatting | bytes 8454144 | tf_op jit(solution)/shard_map/reshape | solution.py:13
  397.1 4.7 fusion.65
  429.5 7.7 %fusion.11 = f32[2048,256]{1,0:T(8,128)} fusion(bf16[16,128,1024]{2,1,0:T(8,128)(2,1)} %copy-done.6, bf16[16,128,1024]{2,1,0:T(8,128)(2,1)} %copy-done.5, f32[16,128,256]{2,1,0:T(8,128)S(1)} %get-tuple-element.41, f32[256]{0:T(256)S(1)} %get-tuple-element.42, f32[256]{0:T(256)S(1)} %get-tuple-element.43, f32[256]{0:T(256)S(1)} %add_rsqrt_fusion, ...), kind=kOutput, calls=%fused_computation.25 | convolution fusion | flops 2172125184 | bytes 14684160 | tf_op jit(solution)/shard_map/rk,ro->ko/dot_general | solution.py:61
  437.2 157.9 %all-reduce.15.cloned.1.call-done = (f32[2048,256]{1,0:T(8,128)}, f32[1024,256]{1,0:T(8,128)}, f32[256,1024]{1,0:T(8,128)}, f32[256,2048]{1,0:T(8,128)}) async-done(((f32[2048,256]{1,0:T(8,128)}, f32[1024,256]{1,0:T(8,128)}, f32[256,1024]{1,0:T(8,128)}, f32[256,2048]{1,0:T(8,128)}), (f32[2048,256]{1,0:T(8,128)}, f32[1024,256]{1,0:T(8,128)}, f32[256,1024]{1,0:T(8,128)}, ...) | async-done | bytes 6291472 | tf_op jit(solution)/shard_map/psum | solution.py:122
  (116 shorter events, 75.2 us)
Async XLA Ops:
  7.2 312.4 %copy-start = (bf16[2048,256]{1,0:T(8,128)(2,1)S(1)}, bf16[2048,256]{1,0:T(8,128)(2,1)}, u32[]{:S(2)}) copy-start(bf16[2048,256]{1,0:T(8,128)(2,1)} %param.10) | copy-start | bytes 3145732
  7.2 5.9 copy-start.21
  7.2 8.5 %copy-start.22 = (s32[16]{0:T(128)S(1)}, s32[16]{0:T(128)}, u32[]{:S(2)}) copy-start(s32[16]{0:T(128)} %param.9) | copy-start | bytes 196
  7.2 159.9 %all-reduce.17.cloned.1.call-start = ((), (), s32[]{:S(2)}) async-start(), calls=%async_computation.4 | async-start | bytes 2097152 | tf_op jit(solution)/shard_map/psum | solution.py:80
  18.4 162.3 %all-to-all-start.1 = ((s32[8,2,2]{1,2,0:T(2,128)}), s32[8,2,2]{1,2,0:T(2,128)S(1)}, u32[]{:S(2)}, u32[]{:S(2)}) async-start(s32[8,2,2]{1,2,0:T(2,128)} %copy.99), calls=%async_computation.1 | async-start | bytes 16384 | tf_op jit(solution)/shard_map/all_to_all | solution.py:89
  167.1 3.2 copy-start.3
  180.7 54.2 %all-to-all-start = ((bf16[16,256,512]{2,1,0:T(8,128)(2,1)}), bf16[16,256,512]{2,1,0:T(8,128)(2,1)}, u32[]{:S(2)}, u32[]{:S(2)}) async-start(bf16[16,256,512]{2,1,0:T(8,128)(2,1)} %gather_fusion), calls=%async_computation | async-start | bytes 8388608 | tf_op jit(solution)/shard_map/all_to_all | solution.py:88
  239.9 6.4 %copy-start.18 = (bf16[256,1024]{1,0:T(8,128)(2,1)S(1)}, bf16[256,1024]{1,0:T(8,128)(2,1)}, u32[]{:S(2)}) copy-start(bf16[256,1024]{1,0:T(8,128)(2,1)} %param.12) | copy-start | bytes 1572868
  239.9 7.4 %copy-start.9 = (bf16[256,2048]{1,0:T(8,128)(2,1)S(1)}, bf16[256,2048]{1,0:T(8,128)(2,1)}, u32[]{:S(2)}) copy-start(bf16[256,2048]{1,0:T(8,128)(2,1)} %param.13) | copy-start | bytes 3145732
  239.9 62.0 %all-to-all-start.2 = ((bf16[16,256,512]{2,1,0:T(8,128)(2,1)}), bf16[16,256,512]{2,1,0:T(8,128)(2,1)}, u32[]{:S(2)}, u32[]{:S(2)}) async-start(bf16[16,256,512]{2,1,0:T(8,128)(2,1)} %gather_fusion.2), calls=%async_computation.2 | async-start | bytes 8388608 | tf_op jit(solution)/shard_map/all_to_all | solution.py:93
  246.0 349.1 %all-reduce.15.cloned.1.call-start = ((), (), s32[]{:S(2)}) async-start(), calls=%async_computation.3 | async-start | bytes 12582912 | tf_op jit(solution)/shard_map/psum | solution.py:122
  319.5 3.2 copy-start.6
  327.4 4.3 copy-start.20
  329.5 3.0 copy-start.13
  329.5 3.0 copy-start.15
  344.7 8.2 %copy-start.2 = (f32[16,128,4,512]{3,1,2,0:T(8,128)}, f32[16,128,4,512]{3,1,2,0:T(8,128)S(1)}, u32[]{:S(2)}) copy-start(f32[16,128,4,512]{3,1,2,0:T(8,128)S(1)} %fusion.24) | copy-start | bytes 50331652
  397.1 4.7 copy-start.7
  397.1 4.7 copy-start.10
  409.7 4.6 copy-start.19
  426.8 2.7 copy-start.4
  595.1 3.2 copy-start.12
  595.1 4.2 copy-start.11
  595.1 5.2 copy-start.8
  595.1 6.5 %copy-start.1 = (bf16[2048,256]{1,0:T(8,128)(2,1)S(1)}, bf16[2048,256]{1,0:T(8,128)(2,1)}, u32[]{:S(2)}) copy-start(bf16[2048,256]{1,0:T(8,128)(2,1)} %param.10) | copy-start | bytes 3145732
  (6 other events, 11.0 us)
Sparse Core Ops, SparseCore 0:
  15.9 151.2 all-reduce.16
  437.3 157.7 all-reduce.14
where the time goes:
time: 618 us; the launch traced here: 609 us
  waiting for transfers between devices  334 us (54%)
  local copies, waits for them, and re-layouts  95.4 us (15%)
  blocking collectives  67.2 us (11%)
  other arithmetic  45.3 us (7%)
  matrix products  34.1 us (6%)
  starting transfers between devices  17.8 us (3%)
  between operations  14.7 us (2%)
    psum x1, waiting for transfers between devices, local(): lax.psum((grad_enc1, grad_enc2, grad_dec1, grad_dec2), ('row', 'col'))  158 us
    psum x1, waiting for transfers between devices, local(): lax.psum((totals, squares, counts), ('row', 'col'))  74.5 us
    psum x1, blocking collectives, local(): lax.psum((totals, squares, counts), ('row', 'col'))  67.2 us
    all_to_all x1, waiting for transfers between devices, local(): lax.all_to_all(payload[ranking], 'col', split_axis=0, concat_axis=0, tile...  53.3 us
    all_to_all x1, waiting for transfers between devices, local(): lax.all_to_all(payload[ranking], 'row', split_axis=0, concat_axis=0, tile...  48.3 us
    reshape x4, local copies, waits for them, and re-layouts, frame_taps(): paired = padded.reshape(windows, length // 2 + 1, 2 * channels)  19.1 us
    another operation x5, other arithmetic, fold_taps(): jnp.stack([even_rows, odd_rows], axis=2)  17 us
    dot_general x4, matrix products, layer_sum(): jnp.einsum('rk,ro->ko', left_flat, right_flat, preferred_element_type=jnp...  14.9 us
  transfers between devices with their start and end apart: 5, of which 4 were waited for; matrix products, arithmetic and copies ran while one was open for 3% of the time, Pallas kernels for 0%

commit v1 on v0

--- a/solution.py
+++ b/solution.py
@@ -77,7 +77,7 @@
     totals = jnp.einsum("ws,wb->sb", table, win_sums, precision=lax.Precision.HIGHEST)
     squares = jnp.einsum("ws,wb->sb", table, win_squares, precision=lax.Precision.HIGHEST)
     counts = jnp.sum(table, axis=0) * frame_count
-    totals, squares, counts = lax.psum((totals, squares, counts), ("row", "col"))
+    totals, squares, counts = lax.psum(lax.psum((totals, squares, counts), "col"), "row")
     center = totals / counts[:, None]
     factor = lax.rsqrt(squares / counts[:, None] - center * center + EPS)
     payload = standardize(log_power, table, center, factor)

time: 618 us -> 691 us (1.12)
  waiting for transfers between devices: 334 us -> 419 us
  blocking collectives: 67.2 us -> 51.6 us
    psum x1 -> x2, waiting for transfers between devices: 74.5 us -> 166 us  [the longest x1 144 us: local(): lax.psum((totals, squares, counts), 'col')]
    psum x1 -> x2, blocking collectives: 67.2 us -> 51.6 us  [the longest x1 34.2 us: local(): lax.psum((totals, squares, counts), 'col')]
    all_to_all x1, starting transfers between devices: 6.14 us -> 13.5 us  [local(): lax.all_to_all(payload[ranking], 'col', split_axis=0, concat_axis=0, tile...]
  transfers between devices with their start and end apart: 5 -> 6, of which waited for: 4 -> 5; matrix products, arithmetic and copies ran while one was open for 3% -> 3% of each run, Pallas kernels for 0% -> 0%
where the time goes in v1:
time: 691 us; the launch traced here: 683 us
  waiting for transfers between devices  419 us (61%)
  local copies, waits for them, and re-layouts  96.2 us (14%)
  blocking collectives  51.6 us (7%)
  other arithmetic  45.3 us (7%)
  matrix products  34.1 us (5%)
  starting transfers between devices  22.5 us (3%)
  between operations  14.4 us (2%)
    psum x1, waiting for transfers between devices, local(): lax.psum((grad_enc1, grad_enc2, grad_dec1, grad_dec2), ('row', 'col'))  157 us
    psum x1, waiting for transfers between devices, local(): lax.psum((totals, squares, counts), 'col')  144 us
    all_to_all x1, waiting for transfers between devices, local(): lax.all_to_all(payload[ranking], 'col', split_axis=0, concat_axis=0, tile...  53.3 us
    all_to_all x1, waiting for transfers between devices, local(): lax.all_to_all(payload[ranking], 'row', split_axis=0, concat_axis=0, tile...  42.1 us
    psum x1, blocking collectives, local(): lax.psum((totals, squares, counts), 'col')  34.2 us
    psum x1, waiting for transfers between devices, local(): lax.psum(lax.psum((totals, squares, counts), 'col'), 'row')  22.2 us
    reshape x4, local copies, waits for them, and re-layouts, frame_taps(): paired = padded.reshape(windows, length // 2 + 1, 2 * channels)  19.1 us
    psum x1, blocking collectives, local(): lax.psum(lax.psum((totals, squares, counts), 'col'), 'row')  17.3 us
  transfers between devices with their start and end apart: 6, of which 5 were waited for; matrix products, arithmetic and copies ran while one was open for 3% of the time, Pallas kernels for 0%

profile of v1, /device:TPU:1, one launch (start us, length us, event | category | flops | bytes accessed | tf_op | source)
XLA Modules:
  0.0 682.7 jit_solution(3585785852350820958)
XLA Ops:
  7.2 5.9 fusion.2
  15.8 143.7 %all-reduce.19.cloned.1.call-done = (f32[256,512]{1,0:T(8,128)}, f32[256,512]{1,0:T(8,128)}) async-done(((f32[256,512]{1,0:T(8,128)}, f32[256,512]{1,0:T(8,128)}), (f32[256,512]{1,0:T(8,128)}, f32[256,512]{1,0:T(8,128)})) %all-reduce.19.cloned.1.call-update) | async-done | bytes 1048592 | tf_op jit(solution)/shard_map/psum | solution.py:80
  166.5 34.2 %psum.72 = f32[256]{0:T(256)S(1)} all-reduce(f32[256]{0:T(256)S(1)} %broadcast_multiply_fusion.3), channel_id=1, replica_groups=mesh['row'=8,'col'=16] {'col'}, use_global_device_ids=true, to_apply=%region_4.0 | all-reduce | flops 256 | bytes 2048 | tf_op jit(solution)/shard_map/psum | solution.py:80
  200.7 17.3 %psum.73 = f32[256]{0:T(256)S(1)} all-reduce(f32[256]{0:T(256)S(1)} %psum.72), channel_id=1, replica_groups=mesh['row'=8,'col'=16] {'row'}, use_global_device_ids=true, to_apply=%region_5.0 | all-reduce | flops 256 | bytes 2048 | tf_op jit(solution)/shard_map/psum | solution.py:80
  218.0 22.2 %all-reduce.21.cloned.1.call-done = (f32[256,512]{1,0:T(8,128)}, f32[256,512]{1,0:T(8,128)}) async-done(((f32[256,512]{1,0:T(8,128)}, f32[256,512]{1,0:T(8,128)}), (f32[256,512]{1,0:T(8,128)}, f32[256,512]{1,0:T(8,128)})) %all-reduce.21.cloned.1.call-update) | async-done | bytes 1048592 | tf_op jit(solution)/shard_map/psum | solution.py:80
  243.4 5.4 multiply_convert_fusion
  248.8 4.9 gather_fusion
  253.8 4.6 all-to-all-start
  259.7 42.1 %all-to-all-done = bf16[16,256,512]{2,1,0:T(8,128)(2,1)} async-done(((bf16[16,256,512]{2,1,0:T(8,128)(2,1)}), bf16[16,256,512]{2,1,0:T(8,128)(2,1)}, u32[]{:S(2)}, u32[]{:S(2)}) %all-to-all-start) | async-done | bytes 4194336 | tf_op jit(solution)/shard_map/all_to_all | solution.py:88
  301.8 4.9 gather_fusion.2
  306.7 13.5 %all-to-all-start.2 = ((bf16[16,256,512]{2,1,0:T(8,128)(2,1)}), bf16[16,256,512]{2,1,0:T(8,128)(2,1)}, u32[]{:S(2)}, u32[]{:S(2)}) async-start(bf16[16,256,512]{2,1,0:T(8,128)(2,1)} %gather_fusion.2), calls=%async_computation.2 | async-start | bytes 8388608 | tf_op jit(solution)/shard_map/all_to_all | solution.py:93
  322.8 53.3 %all-to-all-done.2 = bf16[16,256,512]{2,1,0:T(8,128)(2,1)} async-done(((bf16[16,256,512]{2,1,0:T(8,128)(2,1)}), bf16[16,256,512]{2,1,0:T(8,128)(2,1)}, u32[]{:S(2)}, u32[]{:S(2)}) %all-to-all-start.2) | async-done | bytes 4194336 | tf_op jit(solution)/shard_map/all_to_all | solution.py:93
  376.2 5.9 pad.20
  382.1 7.2 %reshape.92 = bf16[16,129,1024]{2,1,0:T(8,128)(2,1)} reshape(bf16[16,258,512]{2,1,0:T(8,128)(2,1)} %pad.20) | data formatting | bytes 8454144 | tf_op jit(solution)/shard_map/reshape | solution.py:13
  418.9 4.8 slice_bitcast_fusion.2
  427.9 11.7 %fusion.10 = (f32[16,128,1,512]{3,1,0,2:T(8,128)}, f32[16,128,1,512]{3,1,0,2:T(8,128)}) fusion(f32[16,128,4,512]{3,1,2,0:T(8,128)} %copy-done.2, f32[16,127,512]{2,1,0:T(8,128)} %get-tuple-element.22, f32[16,127,512]{2,1,0:T(8,128)} %get-tuple-element.23), kind=kLoop, calls=%fused_computation.24 | loop fusion | flops 2097152 | bytes 25100288 | tf_op jit(solution)/shard_map/stack | solution.py:24
  439.6 4.5 pad_maximum_fusion.1
  444.0 4.9 copy.111
  448.9 10.0 %fusion.1 = bf16[16,256,512]{2,1,0:T(8,128)(2,1)} fusion(f32[16,256,512]{2,0,1:T(8,128)S(1)} %bitcast.146, bf16[16,256,512]{2,1,0:T(8,128)(2,1)} %all-to-all-done.2), kind=kLoop, calls=%fused_computation.8 | loop fusion | flops 8388608 | bytes 16777216 | tf_op jit(solution)/shard_map/convert_element_type | solution.py:109
  458.9 5.9 pad.22
  464.8 7.2 %reshape.95 = bf16[16,129,1024]{2,1,0:T(8,128)(2,1)} reshape(bf16[16,258,512]{2,1,0:T(8,128)(2,1)} %pad.22) | data formatting | bytes 8454144 | tf_op jit(solution)/shard_map/reshape | solution.py:13
  472.0 4.7 fusion.65
  504.5 7.7 %fusion.11 = f32[2048,256]{1,0:T(8,128)} fusion(bf16[16,128,1024]{2,1,0:T(8,128)(2,1)} %copy-done.6, bf16[16,128,1024]{2,1,0:T(8,128)(2,1)} %copy-done.5, f32[16,128,256]{2,1,0:T(8,128)S(1)} %get-tuple-element.43, f32[256]{0:T(256)S(1)} %get-tuple-element.44, f32[256]{0:T(256)S(1)} %get-tuple-element.45, f32[256]{0:T(256)S(1)} %add_rsqrt_fusion, ...), kind=kOutput, calls=%fused_computation.25 | convolution fusion | flops 2172125184 | bytes 14684160 | tf_op jit(solution)/shard_map/rk,ro->ko/dot_general | solution.py:61
  512.2 157.4 %all-reduce.17.cloned.1.call-done = (f32[2048,256]{1,0:T(8,128)}, f32[1024,256]{1,0:T(8,128)}, f32[256,1024]{1,0:T(8,128)}, f32[256,2048]{1,0:T(8,128)}) async-done(((f32[2048,256]{1,0:T(8,128)}, f32[1024,256]{1,0:T(8,128)}, f32[256,1024]{1,0:T(8,128)}, f32[256,2048]{1,0:T(8,128)}), (f32[2048,256]{1,0:T(8,128)}, f32[1024,256]{1,0:T(8,128)}, f32[256,1024]{1,0:T(8,128)}, ...) | async-done | bytes 6291472 | tf_op jit(solution)/shard_map/psum | solution.py:122
  (120 shorter events, 84.5 us)
Async XLA Ops:
  7.2 386.6 %copy-start = (bf16[2048,256]{1,0:T(8,128)(2,1)S(1)}, bf16[2048,256]{1,0:T(8,128)(2,1)}, u32[]{:S(2)}) copy-start(bf16[2048,256]{1,0:T(8,128)(2,1)} %param.10) | copy-start | bytes 3145732
  7.2 6.0 copy-start.21
  7.2 152.3 %copy-start.22 = (s32[16]{0:T(128)S(1)}, s32[16]{0:T(128)}, u32[]{:S(2)}) copy-start(s32[16]{0:T(128)} %param.9) | copy-start | bytes 196
  7.2 152.3 %all-reduce.19.cloned.1.call-start = ((), (), s32[]{:S(2)}) async-start(), calls=%async_computation.4 | async-start | bytes 2097152 | tf_op jit(solution)/shard_map/psum | solution.py:80
  15.7 224.4 %all-reduce.21.cloned.1.call-start = ((), (), s32[]{:S(2)}) async-start(), calls=%async_computation.5 | async-start | bytes 2097152 | tf_op jit(solution)/shard_map/psum | solution.py:80
  162.2 91.6 %all-to-all-start.1 = ((s32[8,2,2]{1,2,0:T(2,128)}), s32[8,2,2]{1,2,0:T(2,128)S(1)}, u32[]{:S(2)}, u32[]{:S(2)}) async-start(s32[8,2,2]{1,2,0:T(2,128)} %copy.99), calls=%async_computation.1 | async-start | bytes 16384 | tf_op jit(solution)/shard_map/all_to_all | solution.py:89
  240.2 3.2 copy-start.3
  253.8 48.0 %all-to-all-start = ((bf16[16,256,512]{2,1,0:T(8,128)(2,1)}), bf16[16,256,512]{2,1,0:T(8,128)(2,1)}, u32[]{:S(2)}, u32[]{:S(2)}) async-start(bf16[16,256,512]{2,1,0:T(8,128)(2,1)} %gather_fusion), calls=%async_computation | async-start | bytes 8388608 | tf_op jit(solution)/shard_map/all_to_all | solution.py:88
  306.7 13.7 %copy-start.18 = (bf16[256,1024]{1,0:T(8,128)(2,1)S(1)}, bf16[256,1024]{1,0:T(8,128)(2,1)}, u32[]{:S(2)}) copy-start(bf16[256,1024]{1,0:T(8,128)(2,1)} %param.12) | copy-start | bytes 1572868
  306.7 14.8 %copy-start.9 = (bf16[256,2048]{1,0:T(8,128)(2,1)S(1)}, bf16[256,2048]{1,0:T(8,128)(2,1)}, u32[]{:S(2)}) copy-start(bf16[256,2048]{1,0:T(8,128)(2,1)} %param.13) | copy-start | bytes 3145732
  306.7 69.4 %all-to-all-start.2 = ((bf16[16,256,512]{2,1,0:T(8,128)(2,1)}), bf16[16,256,512]{2,1,0:T(8,128)(2,1)}, u32[]{:S(2)}, u32[]{:S(2)}) async-start(bf16[16,256,512]{2,1,0:T(8,128)(2,1)} %gather_fusion.2), calls=%async_computation.2 | async-start | bytes 8388608 | tf_op jit(solution)/shard_map/all_to_all | solution.py:93
  320.2 349.3 %all-reduce.17.cloned.1.call-start = ((), (), s32[]{:S(2)}) async-start(), calls=%async_computation.3 | async-start | bytes 12582912 | tf_op jit(solution)/shard_map/psum | solution.py:122
  393.7 3.2 copy-start.6
  401.6 4.3 copy-start.20
  403.7 3.0 copy-start.13
  403.8 3.0 copy-start.15
  418.9 9.0 %copy-start.2 = (f32[16,128,4,512]{3,1,2,0:T(8,128)}, f32[16,128,4,512]{3,1,2,0:T(8,128)S(1)}, u32[]{:S(2)}) copy-start(f32[16,128,4,512]{3,1,2,0:T(8,128)S(1)} %fusion.24) | copy-start | bytes 50331652
  472.0 4.7 copy-start.7
  472.0 4.7 copy-start.10
  484.7 4.6 copy-start.19
  669.5 3.2 copy-start.12
  669.5 4.2 copy-start.11
  669.5 5.2 copy-start.8
  669.5 6.5 copy-start.1
  (7 other events, 13.7 us)
Sparse Core Ops, SparseCore 0:
  15.9 143.5 all-reduce.18
  162.2 77.9 all-reduce.20
  512.3 157.1 all-reduce.16
